TPU v7x, 32 devices: a whole 2x2x4 slice. The times are simulated.
32 devices in a mesh: gr: 4 (over z), gc: 8 (over y, x, core).
Axes of the slice: x: 2, y: 2, z: 4, core: 2. Of those that a mesh axis runs over, the one named last changes fastest.
Arguments:
- student: bfloat16 [4096, 1024], P(('gr', 'gc')), may hold values from -500 to 500
- teacher: bfloat16 [4096, 1024], P(('gr', 'gc')), may hold values from -500 to 500
Outputs:
- student_grad: float32 [4096, 1024], P(('gr', 'gc'))
All inputs are finite; a program needn't handle non-finite values.
Results may differ from a plain program's by a relative error of at most 0.0085.
Values may be sent and summed in bfloat16 or wider, within the bound.
No kernel may reach another device: no remote copies, remote signals or barrier semaphores. Data moves between devices by JAX's collectives and lax.ppermute only.
A program may use at most 64 MiB of HBM per device.

v0:
```python
import functools

import jax
import jax.numpy as jnp
from jax import lax
from jax.experimental import pallas as pl
from jax.experimental.pallas import tpu as pltpu
from jax.sharding import PartitionSpec as P


F32, BF16 = jnp.float32, jnp.bfloat16
VM = pl.BlockSpec(memory_space=pltpu.VMEM)


def inverse_rms(values):
    return lax.rsqrt(jnp.mean(values * values, axis=-1, keepdims=True) + 1e-06)


def unit_of(rows):
    values = rows.astype(F32)
    return (values * inverse_rms(values) * rows.shape[-1] ** (-0.5)).astype(BF16)


def nt(a, b):
    return lax.dot_general(a, b, (((1,), (1,)), ((), ())), preferred_element_type=F32)


def tn(a, b):
    return lax.dot_general(a, b, (((0,), (0,)), ((), ())), preferred_element_type=F32)


def nn(a, b):
    return lax.dot_general(a, b, (((1,), (0,)), ((), ())), preferred_element_type=F32)


def call(kernel, outs, *args, flops=0):
    size = sum(a.size * a.dtype.itemsize for a in args)
    size += sum(o.size * o.dtype.itemsize for o in outs)
    return pl.pallas_call(
        kernel,
        out_shape=outs,
        in_specs=[VM] * len(args),
        out_specs=[VM] * len(outs),
        cost_estimate=pl.CostEstimate(flops=flops, bytes_accessed=size, transcendentals=0),
        compiler_params=pltpu.CompilerParams(vmem_limit_bytes=24 << 20),
    )(*args)


def shape(rows, cols, dtype):
    return jax.ShapeDtypeStruct((rows, cols), dtype)


def block_kernel(n, *refs):
    raw_s, raw_t = refs[:n], refs[n : 2 * n]
    block_s, block_t, pull = refs[2 * n :]
    rows = raw_s[0].shape[0]
    stretch = 0.5 * raw_s[0].shape[1] ** 0.5
    for k in range(n):
        block_s[pl.ds(k * rows, rows), :] = unit_of(raw_s[k][...])
        block_t[pl.ds(k * rows, rows), :] = unit_of(raw_t[k][...])
    own_s, own_t = block_s[pl.ds(0, rows), :], block_t[pl.ds(0, rows), :]
    sim = nt(own_s, block_s[...]) - nt(own_t, block_t[...])
    mismatch = jnp.tanh(stretch * sim).astype(BF16)
    pull[...] = nn(mismatch, block_s[...])


def pair_kernel(n_once, n_both, chunk, *refs):
    block_s, block_t = refs[:2]
    n = n_once + n_both
    raw_s, raw_t = refs[2 : 2 + n], refs[2 + n : 2 + 2 * n]
    outs = refs[2 + 2 * n :]
    back, keep, send = outs[:n_once], outs[n_once], outs[n_once + 1]
    rows, width = raw_s[0].shape
    stretch = 0.5 * width**0.5
    other_s = jnp.concatenate([unit_of(r[...]) for r in raw_s], axis=0)
    other_t = jnp.concatenate([unit_of(r[...]) for r in raw_t], axis=0)
    total = block_s.shape[0]
    half = total // 2
    sums = [None] * n_once
    for start in range(total - chunk, -1, -chunk):
        piece_s = block_s[pl.ds(start, chunk), :]
        piece_t = block_t[pl.ds(start, chunk), :]
        sim = nt(piece_s, other_s) - nt(piece_t, other_t)
        mismatch = jnp.tanh(stretch * sim).astype(BF16)
        part = nn(mismatch, other_s)
        if start >= half:
            send[pl.ds(start - half, chunk), :] = part.astype(BF16)
        else:
            keep[pl.ds(start, chunk), :] = part
        for i in range(n_once):
            term = tn(mismatch[:, i * rows : (i + 1) * rows], piece_s)
            sums[i] = term if sums[i] is None else sums[i] + term
    for i in range(n_once):
        back[i][...] = sums[i].astype(BF16)


def merge_kernel(keep, came, *outs):
    rows = outs[0].shape[0]
    for k, out in enumerate(outs):
        at = pl.ds(k * rows, rows)
        out[...] = (keep[at, :] + came[at, :].astype(F32)).astype(out.dtype)


def end_kernel(factor, student, *refs):
    terms, out = refs[:-1], refs[-1]
    values = student[...].astype(F32)
    inverse = inverse_rms(values)
    unit = (values * inverse * values.shape[-1] ** (-0.5)).astype(BF16).astype(F32)
    pull = terms[0][...]
    for term in terms[1:]:
        pull = pull + term[...].astype(F32)
    radial = jnp.sum(unit * pull, axis=-1, keepdims=True)
    out[...] = factor * inverse * (pull - radial * unit)


def local(n_gr, n_gc, student, teacher):
    rows, width = student.shape
    axes = ("gr", "gc")

    def shift(x, pairs):
        return lax.ppermute(x, axes, pairs)

    def across(x, mask):
        pairs = [(g * n_gc + c, g * n_gc + (c ^ mask)) for g in range(n_gr) for c in range(n_gc)]
        return shift(x, pairs)

    order = []
    for i in range(n_gr):
        order.append(i // 2 if i % 2 == 0 else n_gr - 1 - i // 2)

    def along(x, step):
        pairs = []
        for i in range(n_gr):
            a, b = order[i], order[(i + step) % n_gr]
            pairs += [(a * n_gc + c, b * n_gc + c) for c in range(n_gc)]
        return shift(x, pairs)

    once = list(range(1, (n_gr + 1) // 2))
    both = [n_gr // 2] if n_gr % 2 == 0 else []
    far_s = [along(student, d) for d in once + both]
    far_t = [along(teacher, d) for d in once + both]

    got_s, got_t = {0: student}, {0: teacher}
    for k in range(2, n_gc, 2):
        high = 1 << (k.bit_length() - 1)
        low = k & -k
        got_s[k] = across(got_s[k ^ high], high)
        got_t[k] = across(got_t[k ^ low], low)
    even = list(range(0, n_gc, 2))
    for k in even:
        got_s[k + 1] = across(got_s[k], 1)
        got_t[k + 1] = across(got_t[k], 1)
    slots = even + [k + 1 for k in even]
    total = rows * n_gc
    block_s, block_t, near = call(
        functools.partial(block_kernel, n_gc),
        [shape(total, width, BF16), shape(total, width, BF16), shape(rows, width, F32)],
        *[got_s[k] for k in slots],
        *[got_t[k] for k in slots],
        flops=6 * rows * total * width,
    )
    n = len(once) + len(both)
    half = total // 2
    outs = call(
        functools.partial(pair_kernel, len(once), len(both), min(256, half)),
        [shape(rows, width, BF16)] * len(once)
        + [shape(half, width, F32), shape(half, width, BF16)],
        block_s,
        block_t,
        *far_s,
        *far_t,
        flops=(6 * n + 2 * len(once)) * rows * total * width,
    )
    back, keep, send = outs[: len(once)], outs[-2], outs[-1]
    home = [along(b, n_gr - d) for b, d in zip(back, once)]
    came = across(send, 1)
    merged = call(
        merge_kernel,
        [shape(rows, width, F32)] + [shape(rows, width, BF16)] * (len(even) - 1),
        keep,
        came,
    )
    terms = [across(m, k) for m, k in zip(merged[1:], even[1:])]
    factor = 12.0 * (width / (rows * n_gr * n_gc)) ** 0.5
    return call(
        functools.partial(end_kernel, factor),
        [shape(rows, width, F32)],
        student,
        near,
        merged[0],
        *terms,
        *home,
    )[0]


def solution(mesh):
    n_gr, n_gc = mesh.shape["gr"], mesh.shape["gc"]
    spec = P(("gr", "gc"), None)

    def body(student, teacher):
        return local(n_gr, n_gc, student, teacher)

    return jax.shard_map(
        body, mesh=mesh, in_specs=(spec, spec), out_specs=spec, check_vma=False
    )
```

profile of v0, /device:TPU:0, one launch (start us, length us, event | category | flops | bytes accessed | tf_op | source)
XLA Modules:
  0.0 74.2 jit_solution(10254238984811534437)
XLA Ops:
  0.0 3.0 %collective-permute-start = (bf16[128,1024]{1,0:T(8,128)(2,1)}, bf16[128,1024]{1,0:T(8,128)(2,1)S(1)}, u32[]{:S(2)}, u32[]{:S(2)}) collective-permute-start(bf16[128,1024]{1,0:T(8,128)(2,1)} %student.1), channel_id=1, source_target_pairs={{0,2},{1,3},{2,0},{3,1},{4,6},{5,7},{6,4},{7,5},{8,10},{9,11},{10,... | collective-permute-start | bytes 786440 | tf_op jit(solution)/shard_map/ppermute | solution.py:121
  3.0 1.5 %collective-permute-start.1 = (bf16[128,1024]{1,0:T(8,128)(2,1)}, bf16[128,1024]{1,0:T(8,128)(2,1)S(1)}, u32[]{:S(2)}, u32[]{:S(2)}) collective-permute-start(bf16[128,1024]{1,0:T(8,128)(2,1)} %student.1), channel_id=1, source_target_pairs={{0,4},{1,5},{2,6},{3,7},{4,0},{5,1},{6,2},{7,3},{8,12},{9,13},{10,... | collective-permute-start | bytes 786440 | tf_op jit(solution)/shard_map/ppermute | solution.py:121
  4.5 0.5 collective-permute-start.8
  5.0 5.3 %collective-permute-done.refs_1_ = bf16[128,1024]{1,0:T(8,128)(2,1)S(1)} collective-permute-done((bf16[128,1024]{1,0:T(8,128)(2,1)}, bf16[128,1024]{1,0:T(8,128)(2,1)S(1)}, u32[]{:S(2)}, u32[]{:S(2)}) %collective-permute-start) | collective-permute-done | bytes 262176 | tf_op jit(solution)/shard_map/ppermute | solution.py:121
  10.3 2.0 %collective-permute-done.1.refs_2_ = bf16[128,1024]{1,0:T(8,128)(2,1)S(1)} collective-permute-done((bf16[128,1024]{1,0:T(8,128)(2,1)}, bf16[128,1024]{1,0:T(8,128)(2,1)S(1)}, u32[]{:S(2)}, u32[]{:S(2)}) %collective-permute-start.1) | collective-permute-done | bytes 262176 | tf_op jit(solution)/shard_map/ppermute | solution.py:121
  12.4 1.5 %collective-permute-start.2 = (bf16[128,1024]{1,0:T(8,128)(2,1)S(1)}, bf16[128,1024]{1,0:T(8,128)(2,1)S(1)}, u32[]{:S(2)}, u32[]{:S(2)}) collective-permute-start(bf16[128,1024]{1,0:T(8,128)(2,1)S(1)} %collective-permute-done.refs_1_), channel_id=1, source_target_pairs={{0,4},{1,5},{2,6},{3,7},{4,0},{5,1},{6,2},{7,3},{8,12},{9,13},{10,... | collective-permute-start | bytes 786440 | tf_op jit(solution)/shard_map/ppermute | solution.py:121
  13.9 4.1 %collective-permute-done.8.refs_10_ = bf16[128,1024]{1,0:T(8,128)(2,1)S(1)} collective-permute-done((bf16[128,1024]{1,0:T(8,128)(2,1)}, bf16[128,1024]{1,0:T(8,128)(2,1)S(1)}, u32[]{:S(2)}, u32[]{:S(2)}) %collective-permute-start.8) | collective-permute-done | bytes 262176 | tf_op jit(solution)/shard_map/ppermute | solution.py:121
  18.0 0.5 collective-permute-start.11
  18.6 3.6 %collective-permute-done.2.refs_3_ = bf16[128,1024]{1,0:T(8,128)(2,1)S(1)} collective-permute-done((bf16[128,1024]{1,0:T(8,128)(2,1)S(1)}, bf16[128,1024]{1,0:T(8,128)(2,1)S(1)}, u32[]{:S(2)}, u32[]{:S(2)}) %collective-permute-start.2) | collective-permute-done | bytes 262176 | tf_op jit(solution)/shard_map/ppermute | solution.py:121
  22.2 0.5 collective-permute-start.6
  22.7 1.6 %collective-permute-done.9.refs_11_ = bf16[128,1024]{1,0:T(8,128)(2,1)S(1)} collective-permute-done((bf16[128,1024]{1,0:T(8,128)(2,1)S(1)}, bf16[128,1024]{1,0:T(8,128)(2,1)S(1)}, u32[]{:S(2)}, u32[]{:S(2)}) %collective-permute-start.9) | collective-permute-done | bytes 262176 | tf_op jit(solution)/shard_map/ppermute | solution.py:121
  24.4 3.6 %collective-permute-start.14 = (bf16[128,1024]{1,0:T(8,128)(2,1)}, bf16[128,1024]{1,0:T(8,128)(2,1)S(1)}, u32[]{:S(2)}, u32[]{:S(2)}) collective-permute-start(bf16[128,1024]{1,0:T(8,128)(2,1)} %student.1), channel_id=1, source_target_pairs={{0,24},{1,25},{2,26},{3,27},{4,28},{5,29},{6,30},{7,31},{24,8},{25... | collective-permute-start | bytes 786440 | tf_op jit(solution)/shard_map/ppermute | solution.py:121
  28.0 0.8 %collective-permute-start.16 = (bf16[128,1024]{1,0:T(8,128)(2,1)}, bf16[128,1024]{1,0:T(8,128)(2,1)S(1)}, u32[]{:S(2)}, u32[]{:S(2)}) collective-permute-start(bf16[128,1024]{1,0:T(8,128)(2,1)} %refs_8_.1), channel_id=1, source_target_pairs={{0,24},{1,25},{2,26},{3,27},{4,28},{5,29},{6,30},{7,31},{24,8},{25... | collective-permute-start | bytes 786440 | tf_op jit(solution)/shard_map/ppermute | solution.py:121
  28.8 1.3 %collective-permute-start.17 = (bf16[128,1024]{1,0:T(8,128)(2,1)}, bf16[128,1024]{1,0:T(8,128)(2,1)S(1)}, u32[]{:S(2)}, u32[]{:S(2)}) collective-permute-start(bf16[128,1024]{1,0:T(8,128)(2,1)} %refs_8_.1), channel_id=1, source_target_pairs={{0,8},{1,9},{2,10},{3,11},{4,12},{5,13},{6,14},{7,15},{24,16},{25,... | collective-permute-start | bytes 786440 | tf_op jit(solution)/shard_map/ppermute | solution.py:121
  30.1 0.9 %copy-done = bf16[128,1024]{1,0:T(8,128)(2,1)S(1)} copy-done((bf16[128,1024]{1,0:T(8,128)(2,1)S(1)}, bf16[128,1024]{1,0:T(8,128)(2,1)}, u32[]{:S(2)}) %copy-start) | copy-done | bytes 262168
  31.0 0.9 %copy-done.2 = bf16[128,1024]{1,0:T(8,128)(2,1)S(1)} copy-done((bf16[128,1024]{1,0:T(8,128)(2,1)S(1)}, bf16[128,1024]{1,0:T(8,128)(2,1)}, u32[]{:S(2)}) %copy-start.2) | copy-done | bytes 262168
  32.0 2.5 %shard_map.28 = (bf16[1024,1024]{1,0:T(8,128)(2,1)S(1)}, bf16[1024,1024]{1,0:T(8,128)(2,1)S(1)}, f32[128,1024]{1,0:T(8,128)S(1)}) custom-call(bf16[128,1024]{1,0:T(8,128)(2,1)S(1)} %copy-done, bf16[128,1024]{1,0:T(8,128)(2,1)S(1)} %collective-permute-done.refs_1_, bf16[128,1024]{1,0:T(8,128)(2,1)S(1)} %collective-permute-done.1.refs_2_, ...), custom_call_target="tpu_custom_call" | custom-call | flops 805306368 | bytes 8912896 | tf_op jit(solution)/shard_map/pallas_call | solution.py:39
  34.4 5.9 %collective-permute-done.14.refs_2_ = bf16[128,1024]{1,0:T(8,128)(2,1)S(1)} collective-permute-done((bf16[128,1024]{1,0:T(8,128)(2,1)}, bf16[128,1024]{1,0:T(8,128)(2,1)S(1)}, u32[]{:S(2)}, u32[]{:S(2)}) %collective-permute-start.14) | collective-permute-done | bytes 262176 | tf_op jit(solution)/shard_map/ppermute | solution.py:121
  40.4 2.6 %collective-permute-done.15.refs_3_ = bf16[128,1024]{1,0:T(8,128)(2,1)S(1)} collective-permute-done((bf16[128,1024]{1,0:T(8,128)(2,1)}, bf16[128,1024]{1,0:T(8,128)(2,1)S(1)}, u32[]{:S(2)}, u32[]{:S(2)}) %collective-permute-start.15) | collective-permute-done | bytes 262176 | tf_op jit(solution)/shard_map/ppermute | solution.py:121
  43.0 8.2 %collective-permute-done.16.refs_4_ = bf16[128,1024]{1,0:T(8,128)(2,1)S(1)} collective-permute-done((bf16[128,1024]{1,0:T(8,128)(2,1)}, bf16[128,1024]{1,0:T(8,128)(2,1)S(1)}, u32[]{:S(2)}, u32[]{:S(2)}) %collective-permute-start.16) | collective-permute-done | bytes 262176 | tf_op jit(solution)/shard_map/ppermute | solution.py:121
  51.2 1.2 %collective-permute-done.17.refs_5_ = bf16[128,1024]{1,0:T(8,128)(2,1)S(1)} collective-permute-done((bf16[128,1024]{1,0:T(8,128)(2,1)}, bf16[128,1024]{1,0:T(8,128)(2,1)S(1)}, u32[]{:S(2)}, u32[]{:S(2)}) %collective-permute-start.17) | collective-permute-done | bytes 262176 | tf_op jit(solution)/shard_map/ppermute | solution.py:121
  52.3 2.8 %shard_map.29 = (bf16[128,1024]{1,0:T(8,128)(2,1)S(1)}, f32[512,1024]{1,0:T(8,128)S(1)}, bf16[512,1024]{1,0:T(8,128)(2,1)S(1)}) custom-call(bf16[1024,1024]{1,0:T(8,128)(2,1)S(1)} %get-tuple-element.16.refs_0_, bf16[1024,1024]{1,0:T(8,128)(2,1)S(1)} %get-tuple-element.17.refs_1_, bf16[128,1024]{1,0:T(8,128)(2,1)S(1)} %collective-permute-done.14.refs_2_, ...), custom_call_target="tpu_custom_call" | custom-call | flops 1879048192 | bytes 8650752 | tf_op jit(solution)/shard_map/pallas_call | solution.py:39
  55.2 0.4 collective-permute-start.22
  55.7 2.2 %collective-permute-done.18.came = bf16[512,1024]{1,0:T(8,128)(2,1)S(1)} collective-permute-done((bf16[512,1024]{1,0:T(8,128)(2,1)S(1)}, bf16[512,1024]{1,0:T(8,128)(2,1)S(1)}, u32[]{:S(2)}, u32[]{:S(2)}) %collective-permute-start.18) | collective-permute-done | bytes 1048608 | tf_op jit(solution)/shard_map/ppermute | solution.py:121
  58.1 0.5 collective-permute-start.19
  58.6 1.6 %collective-permute-start.20 = (bf16[128,1024]{1,0:T(8,128)(2,1)S(1)}, bf16[128,1024]{1,0:T(8,128)(2,1)S(1)}, u32[]{:S(2)}, u32[]{:S(2)}) collective-permute-start(bf16[128,1024]{1,0:T(8,128)(2,1)S(1)} %get-tuple-element.22), channel_id=1, source_target_pairs={{0,4},{1,5},{2,6},{3,7},{4,0},{5,1},{6,2},{7,3},{8,12},{9,13},{10,... | collective-permute-start | bytes 786440 | tf_op jit(solution)/shard_map/ppermute | solution.py:121
  60.2 1.4 %collective-permute-start.21 = (bf16[128,1024]{1,0:T(8,128)(2,1)S(1)}, bf16[128,1024]{1,0:T(8,128)(2,1)S(1)}, u32[]{:S(2)}, u32[]{:S(2)}) collective-permute-start(bf16[128,1024]{1,0:T(8,128)(2,1)S(1)} %get-tuple-element.23), channel_id=1, source_target_pairs={{0,6},{1,7},{2,4},{3,5},{4,2},{5,3},{6,0},{7,1},{8,14},{9,15},{10,... | collective-permute-start | bytes 786440 | tf_op jit(solution)/shard_map/ppermute | solution.py:121
  61.6 4.2 %collective-permute-done.22.refs_5_ = bf16[128,1024]{1,0:T(8,128)(2,1)S(1)} collective-permute-done((bf16[128,1024]{1,0:T(8,128)(2,1)S(1)}, bf16[128,1024]{1,0:T(8,128)(2,1)S(1)}, u32[]{:S(2)}, u32[]{:S(2)}) %collective-permute-start.22) | collective-permute-done | bytes 262176 | tf_op jit(solution)/shard_map/ppermute | solution.py:121
  65.8 1.5 %collective-permute-done.19.refs_2_ = bf16[128,1024]{1,0:T(8,128)(2,1)S(1)} collective-permute-done((bf16[128,1024]{1,0:T(8,128)(2,1)S(1)}, bf16[128,1024]{1,0:T(8,128)(2,1)S(1)}, u32[]{:S(2)}, u32[]{:S(2)}) %collective-permute-start.19) | collective-permute-done | bytes 262176 | tf_op jit(solution)/shard_map/ppermute | solution.py:121
  67.3 4.1 %collective-permute-done.20.refs_3_ = bf16[128,1024]{1,0:T(8,128)(2,1)S(1)} collective-permute-done((bf16[128,1024]{1,0:T(8,128)(2,1)S(1)}, bf16[128,1024]{1,0:T(8,128)(2,1)S(1)}, u32[]{:S(2)}, u32[]{:S(2)}) %collective-permute-start.20) | collective-permute-done | bytes 262176 | tf_op jit(solution)/shard_map/ppermute | solution.py:121
  71.4 1.6 %collective-permute-done.21.refs_4_ = bf16[128,1024]{1,0:T(8,128)(2,1)S(1)} collective-permute-done((bf16[128,1024]{1,0:T(8,128)(2,1)S(1)}, bf16[128,1024]{1,0:T(8,128)(2,1)S(1)}, u32[]{:S(2)}, u32[]{:S(2)}) %collective-permute-start.21) | collective-permute-done | bytes 262176 | tf_op jit(solution)/shard_map/ppermute | solution.py:121
  73.0 1.2 %shard_map.31 = f32[128,1024]{1,0:T(8,128)} custom-call(bf16[128,1024]{1,0:T(8,128)(2,1)S(1)} %copy-done.1, f32[128,1024]{1,0:T(8,128)S(1)} %get-tuple-element.15.refs_0_, f32[128,1024]{1,0:T(8,128)S(1)} %get-tuple-element.20.refs_1_, bf16[128,1024]{1,0:T(8,128)(2,1)S(1)} %collective-permute-done.19.refs_2_, ...), custom_call_target="tpu_custom_call" | custom-call | bytes 2883584 | tf_op jit(solution)/shard_map/pallas_call | solution.py:39
  (24 shorter events, 0.4 us)
Async XLA Ops:
  0.0 10.3 %collective-permute-start = (bf16[128,1024]{1,0:T(8,128)(2,1)}, bf16[128,1024]{1,0:T(8,128)(2,1)S(1)}, u32[]{:S(2)}, u32[]{:S(2)}) collective-permute-start(bf16[128,1024]{1,0:T(8,128)(2,1)} %student.1), channel_id=1, source_target_pairs={{0,2},{1,3},{2,0},{3,1},{4,6},{5,7},{6,4},{7,5},{8,10},{9,11},{10,... | collective-permute-start | bytes 786440 | tf_op jit(solution)/shard_map/ppermute | solution.py:121
  3.0 9.4 %collective-permute-start.1 = (bf16[128,1024]{1,0:T(8,128)(2,1)}, bf16[128,1024]{1,0:T(8,128)(2,1)S(1)}, u32[]{:S(2)}, u32[]{:S(2)}) collective-permute-start(bf16[128,1024]{1,0:T(8,128)(2,1)} %student.1), channel_id=1, source_target_pairs={{0,4},{1,5},{2,6},{3,7},{4,0},{5,1},{6,2},{7,3},{8,12},{9,13},{10,... | collective-permute-start | bytes 786440 | tf_op jit(solution)/shard_map/ppermute | solution.py:121
  4.5 9.4 %collective-permute-start.3 = (bf16[128,1024]{1,0:T(8,128)(2,1)}, bf16[128,1024]{1,0:T(8,128)(2,1)S(1)}, u32[]{:S(2)}, u32[]{:S(2)}) collective-permute-start(bf16[128,1024]{1,0:T(8,128)(2,1)} %student.1), channel_id=1, source_target_pairs={{0,1},{1,0},{2,3},{3,2},{4,5},{5,4},{6,7},{7,6},{8,9},{9,8},{10,11... | collective-permute-start | bytes 786440 | tf_op jit(solution)/shard_map/ppermute | solution.py:121
  4.5 13.5 %collective-permute-start.8 = (bf16[128,1024]{1,0:T(8,128)(2,1)}, bf16[128,1024]{1,0:T(8,128)(2,1)S(1)}, u32[]{:S(2)}, u32[]{:S(2)}) collective-permute-start(bf16[128,1024]{1,0:T(8,128)(2,1)} %refs_8_.1), channel_id=1, source_target_pairs={{0,4},{1,5},{2,6},{3,7},{4,0},{5,1},{6,2},{7,3},{8,12},{9,13},{10,... | collective-permute-start | bytes 786440 | tf_op jit(solution)/shard_map/ppermute | solution.py:121
  5.0 13.0 %collective-permute-start.7 = (bf16[128,1024]{1,0:T(8,128)(2,1)}, bf16[128,1024]{1,0:T(8,128)(2,1)S(1)}, u32[]{:S(2)}, u32[]{:S(2)}) collective-permute-start(bf16[128,1024]{1,0:T(8,128)(2,1)} %refs_8_.1), channel_id=1, source_target_pairs={{0,2},{1,3},{2,0},{3,1},{4,6},{5,7},{6,4},{7,5},{8,10},{9,11},{10,... | collective-permute-start | bytes 786440 | tf_op jit(solution)/shard_map/ppermute | solution.py:121
  10.3 7.7 %collective-permute-start.10 = (bf16[128,1024]{1,0:T(8,128)(2,1)}, bf16[128,1024]{1,0:T(8,128)(2,1)S(1)}, u32[]{:S(2)}, u32[]{:S(2)}) collective-permute-start(bf16[128,1024]{1,0:T(8,128)(2,1)} %refs_8_.1), channel_id=1, source_target_pairs={{0,1},{1,0},{2,3},{3,2},{4,5},{5,4},{6,7},{7,6},{8,9},{9,8},{10,11... | collective-permute-start | bytes 786440 | tf_op jit(solution)/shard_map/ppermute | solution.py:121
  12.4 9.8 %collective-permute-start.2 = (bf16[128,1024]{1,0:T(8,128)(2,1)S(1)}, bf16[128,1024]{1,0:T(8,128)(2,1)S(1)}, u32[]{:S(2)}, u32[]{:S(2)}) collective-permute-start(bf16[128,1024]{1,0:T(8,128)(2,1)S(1)} %collective-permute-done.refs_1_), channel_id=1, source_target_pairs={{0,4},{1,5},{2,6},{3,7},{4,0},{5,1},{6,2},{7,3},{8,12},{9,13},{10,... | collective-permute-start | bytes 786440 | tf_op jit(solution)/shard_map/ppermute | solution.py:121
  13.9 8.3 %collective-permute-start.4 = (bf16[128,1024]{1,0:T(8,128)(2,1)S(1)}, bf16[128,1024]{1,0:T(8,128)(2,1)S(1)}, u32[]{:S(2)}, u32[]{:S(2)}) collective-permute-start(bf16[128,1024]{1,0:T(8,128)(2,1)S(1)} %collective-permute-done.refs_1_), channel_id=1, source_target_pairs={{0,1},{1,0},{2,3},{3,2},{4,5},{5,4},{6,7},{7,6},{8,9},{9,8},{10,11... | collective-permute-start | bytes 786440 | tf_op jit(solution)/shard_map/ppermute | solution.py:121
  18.0 6.4 %collective-permute-start.9 = (bf16[128,1024]{1,0:T(8,128)(2,1)S(1)}, bf16[128,1024]{1,0:T(8,128)(2,1)S(1)}, u32[]{:S(2)}, u32[]{:S(2)}) collective-permute-start(bf16[128,1024]{1,0:T(8,128)(2,1)S(1)} %collective-permute-done.8.refs_10_), channel_id=1, source_target_pairs={{0,2},{1,3},{2,0},{3,1},{4,6},{5,7},{6,4},{7,5},{8,10},{9,11},{10,... | collective-permute-start | bytes 786440 | tf_op jit(solution)/shard_map/ppermute | solution.py:121
  18.0 6.3 %collective-permute-start.5 = (bf16[128,1024]{1,0:T(8,128)(2,1)S(1)}, bf16[128,1024]{1,0:T(8,128)(2,1)S(1)}, u32[]{:S(2)}, u32[]{:S(2)}) collective-permute-start(bf16[128,1024]{1,0:T(8,128)(2,1)S(1)} %collective-permute-done.1.refs_2_), channel_id=1, source_target_pairs={{0,1},{1,0},{2,3},{3,2},{4,5},{5,4},{6,7},{7,6},{8,9},{9,8},{10,11... | collective-permute-start | bytes 786440 | tf_op jit(solution)/shard_map/ppermute | solution.py:121
  18.0 9.9 %collective-permute-start.11 = (bf16[128,1024]{1,0:T(8,128)(2,1)S(1)}, bf16[128,1024]{1,0:T(8,128)(2,1)S(1)}, u32[]{:S(2)}, u32[]{:S(2)}) collective-permute-start(bf16[128,1024]{1,0:T(8,128)(2,1)S(1)} %collective-permute-done.7.refs_9_), channel_id=1, source_target_pairs={{0,1},{1,0},{2,3},{3,2},{4,5},{5,4},{6,7},{7,6},{8,9},{9,8},{10,11... | collective-permute-start | bytes 786440 | tf_op jit(solution)/shard_map/ppermute | solution.py:121
  22.2 5.8 %collective-permute-start.12 = (bf16[128,1024]{1,0:T(8,128)(2,1)S(1)}, bf16[128,1024]{1,0:T(8,128)(2,1)S(1)}, u32[]{:S(2)}, u32[]{:S(2)}) collective-permute-start(bf16[128,1024]{1,0:T(8,128)(2,1)S(1)} %collective-permute-done.8.refs_10_), channel_id=1, source_target_pairs={{0,1},{1,0},{2,3},{3,2},{4,5},{5,4},{6,7},{7,6},{8,9},{9,8},{10,11... | collective-permute-start | bytes 786440 | tf_op jit(solution)/shard_map/ppermute | solution.py:121
  22.2 6.6 %collective-permute-start.6 = (bf16[128,1024]{1,0:T(8,128)(2,1)S(1)}, bf16[128,1024]{1,0:T(8,128)(2,1)S(1)}, u32[]{:S(2)}, u32[]{:S(2)}) collective-permute-start(bf16[128,1024]{1,0:T(8,128)(2,1)S(1)} %collective-permute-done.2.refs_3_), channel_id=1, source_target_pairs={{0,1},{1,0},{2,3},{3,2},{4,5},{5,4},{6,7},{7,6},{8,9},{9,8},{10,11... | collective-permute-start | bytes 786440 | tf_op jit(solution)/shard_map/ppermute | solution.py:121
  24.3 5.7 %collective-permute-start.13 = (bf16[128,1024]{1,0:T(8,128)(2,1)S(1)}, bf16[128,1024]{1,0:T(8,128)(2,1)S(1)}, u32[]{:S(2)}, u32[]{:S(2)}) collective-permute-start(bf16[128,1024]{1,0:T(8,128)(2,1)S(1)} %collective-permute-done.9.refs_11_), channel_id=1, source_target_pairs={{0,1},{1,0},{2,3},{3,2},{4,5},{5,4},{6,7},{7,6},{8,9},{9,8},{10,11... | collective-permute-start | bytes 786440 | tf_op jit(solution)/shard_map/ppermute | solution.py:121
  24.4 16.0 %collective-permute-start.14 = (bf16[128,1024]{1,0:T(8,128)(2,1)}, bf16[128,1024]{1,0:T(8,128)(2,1)S(1)}, u32[]{:S(2)}, u32[]{:S(2)}) collective-permute-start(bf16[128,1024]{1,0:T(8,128)(2,1)} %student.1), channel_id=1, source_target_pairs={{0,24},{1,25},{2,26},{3,27},{4,28},{5,29},{6,30},{7,31},{24,8},{25... | collective-permute-start | bytes 786440 | tf_op jit(solution)/shard_map/ppermute | solution.py:121
  28.0 15.0 %collective-permute-start.15 = (bf16[128,1024]{1,0:T(8,128)(2,1)}, bf16[128,1024]{1,0:T(8,128)(2,1)S(1)}, u32[]{:S(2)}, u32[]{:S(2)}) collective-permute-start(bf16[128,1024]{1,0:T(8,128)(2,1)} %student.1), channel_id=1, source_target_pairs={{0,8},{1,9},{2,10},{3,11},{4,12},{5,13},{6,14},{7,15},{24,16},{25,... | collective-permute-start | bytes 786440 | tf_op jit(solution)/shard_map/ppermute | solution.py:121
  28.0 23.2 %collective-permute-start.16 = (bf16[128,1024]{1,0:T(8,128)(2,1)}, bf16[128,1024]{1,0:T(8,128)(2,1)S(1)}, u32[]{:S(2)}, u32[]{:S(2)}) collective-permute-start(bf16[128,1024]{1,0:T(8,128)(2,1)} %refs_8_.1), channel_id=1, source_target_pairs={{0,24},{1,25},{2,26},{3,27},{4,28},{5,29},{6,30},{7,31},{24,8},{25... | collective-permute-start | bytes 786440 | tf_op jit(solution)/shard_map/ppermute | solution.py:121
  28.8 23.6 %collective-permute-start.17 = (bf16[128,1024]{1,0:T(8,128)(2,1)}, bf16[128,1024]{1,0:T(8,128)(2,1)S(1)}, u32[]{:S(2)}, u32[]{:S(2)}) collective-permute-start(bf16[128,1024]{1,0:T(8,128)(2,1)} %refs_8_.1), channel_id=1, source_target_pairs={{0,8},{1,9},{2,10},{3,11},{4,12},{5,13},{6,14},{7,15},{24,16},{25,... | collective-permute-start | bytes 786440 | tf_op jit(solution)/shard_map/ppermute | solution.py:121
  30.1 1.0 %copy-start = (bf16[128,1024]{1,0:T(8,128)(2,1)S(1)}, bf16[128,1024]{1,0:T(8,128)(2,1)}, u32[]{:S(2)}) copy-start(bf16[128,1024]{1,0:T(8,128)(2,1)} %student.1) | copy-start | bytes 786436
  31.0 0.9 %copy-start.2 = (bf16[128,1024]{1,0:T(8,128)(2,1)S(1)}, bf16[128,1024]{1,0:T(8,128)(2,1)}, u32[]{:S(2)}) copy-start(bf16[128,1024]{1,0:T(8,128)(2,1)} %refs_8_.1) | copy-start | bytes 786436
  55.1 17.9 %copy-start.1 = (bf16[128,1024]{1,0:T(8,128)(2,1)S(1)}, bf16[128,1024]{1,0:T(8,128)(2,1)}, u32[]{:S(2)}) copy-start(bf16[128,1024]{1,0:T(8,128)(2,1)} %student.1) | copy-start | bytes 786436
  55.1 2.7 %collective-permute-start.18 = (bf16[512,1024]{1,0:T(8,128)(2,1)S(1)}, bf16[512,1024]{1,0:T(8,128)(2,1)S(1)}, u32[]{:S(2)}, u32[]{:S(2)}) collective-permute-start(bf16[512,1024]{1,0:T(8,128)(2,1)S(1)} %get-tuple-element.19), channel_id=1, source_target_pairs={{0,1},{1,0},{2,3},{3,2},{4,5},{5,4},{6,7},{7,6},{8,9},{9,8},{10,11... | collective-permute-start | bytes 3145736 | tf_op jit(solution)/shard_map/ppermute | solution.py:121
  55.2 10.6 %collective-permute-start.22 = (bf16[128,1024]{1,0:T(8,128)(2,1)S(1)}, bf16[128,1024]{1,0:T(8,128)(2,1)S(1)}, u32[]{:S(2)}, u32[]{:S(2)}) collective-permute-start(bf16[128,1024]{1,0:T(8,128)(2,1)S(1)} %get-tuple-element.24), channel_id=1, source_target_pairs={{0,16},{1,17},{2,18},{3,19},{4,20},{5,21},{6,22},{7,23},{24,0},{25... | collective-permute-start | bytes 786440 | tf_op jit(solution)/shard_map/ppermute | solution.py:121
  58.1 9.2 %collective-permute-start.19 = (bf16[128,1024]{1,0:T(8,128)(2,1)S(1)}, bf16[128,1024]{1,0:T(8,128)(2,1)S(1)}, u32[]{:S(2)}, u32[]{:S(2)}) collective-permute-start(bf16[128,1024]{1,0:T(8,128)(2,1)S(1)} %get-tuple-element.21), channel_id=1, source_target_pairs={{0,2},{1,3},{2,0},{3,1},{4,6},{5,7},{6,4},{7,5},{8,10},{9,11},{10,... | collective-permute-start | bytes 786440 | tf_op jit(solution)/shard_map/ppermute | solution.py:121
  58.6 12.8 %collective-permute-start.20 = (bf16[128,1024]{1,0:T(8,128)(2,1)S(1)}, bf16[128,1024]{1,0:T(8,128)(2,1)S(1)}, u32[]{:S(2)}, u32[]{:S(2)}) collective-permute-start(bf16[128,1024]{1,0:T(8,128)(2,1)S(1)} %get-tuple-element.22), channel_id=1, source_target_pairs={{0,4},{1,5},{2,6},{3,7},{4,0},{5,1},{6,2},{7,3},{8,12},{9,13},{10,... | collective-permute-start | bytes 786440 | tf_op jit(solution)/shard_map/ppermute | solution.py:121
  60.2 12.9 %collective-permute-start.21 = (bf16[128,1024]{1,0:T(8,128)(2,1)S(1)}, bf16[128,1024]{1,0:T(8,128)(2,1)S(1)}, u32[]{:S(2)}, u32[]{:S(2)}) collective-permute-start(bf16[128,1024]{1,0:T(8,128)(2,1)S(1)} %get-tuple-element.23), channel_id=1, source_target_pairs={{0,6},{1,7},{2,4},{3,5},{4,2},{5,3},{6,0},{7,1},{8,14},{9,15},{10,... | collective-permute-start | bytes 786440 | tf_op jit(solution)/shard_map/ppermute | solution.py:121
where the time goes:
time: 74.4 us; the launch traced here: 74.2 us
  waiting for transfers between devices  48.2 us (65%)
  starting transfers between devices  17.4 us (23%)
  Pallas kernels  6.61 us (9%)
  local copies, waits for them, and re-layouts  1.91 us (3%)
    ppermute x23, waiting for transfers between devices, shift(): return lax.ppermute(x, axes, pairs)  48.2 us
    ppermute x23, starting transfers between devices, shift(): return lax.ppermute(x, axes, pairs)  17.4 us
    pallas_call x4, Pallas kernels, call(): pl.pallas_call(kernel, out_shape=outs, in_specs=[VM] * len(args), out_spe...  6.61 us
    unnamed x6, local copies, waits for them, and re-layouts  1.91 us
  transfers between devices with their start and end apart: 23, of which 14 were waited for; matrix products, arithmetic and copies ran while one was open for 0% of the time, Pallas kernels for 4%

commit v1 on v0

v1 whole, which is shorter than its diff:
```python
import functools

import jax
import jax.numpy as jnp
from jax import lax
from jax.experimental import pallas as pl
from jax.experimental.pallas import tpu as pltpu
from jax.sharding import PartitionSpec as P


F32, BF16 = jnp.float32, jnp.bfloat16
VM = pl.BlockSpec(memory_space=pltpu.VMEM)


def inverse_rms(values):
    return lax.rsqrt(jnp.mean(values * values, axis=-1, keepdims=True) + 1e-06)


def unit_of(rows):
    values = rows.astype(F32)
    return (values * inverse_rms(values) * rows.shape[-1] ** (-0.5)).astype(BF16)


def nt(a, b):
    return lax.dot_general(a, b, (((1,), (1,)), ((), ())), preferred_element_type=F32)


def tn(a, b):
    return lax.dot_general(a, b, (((0,), (0,)), ((), ())), preferred_element_type=F32)


def nn(a, b):
    return lax.dot_general(a, b, (((1,), (0,)), ((), ())), preferred_element_type=F32)


def call(kernel, outs, *args, flops=0):
    size = sum(a.size * a.dtype.itemsize for a in args)
    size += sum(o.size * o.dtype.itemsize for o in outs)
    return pl.pallas_call(
        kernel,
        out_shape=outs,
        in_specs=[VM] * len(args),
        out_specs=[VM] * len(outs),
        cost_estimate=pl.CostEstimate(flops=flops, bytes_accessed=size, transcendentals=0),
        compiler_params=pltpu.CompilerParams(vmem_limit_bytes=24 << 20),
    )(*args)


def shape(rows, cols, dtype):
    return jax.ShapeDtypeStruct((rows, cols), dtype)


def store_units(outs, raws):
    n = len(raws) // len(outs)
    for i, raw in enumerate(raws):
        rows = raw.shape[0]
        outs[i // n][pl.ds(i % n * rows, rows), :] = unit_of(raw[...])


def pull_of(rows_s, rows_t, *block):
    stretch = 0.5 * rows_s.shape[1] ** 0.5
    total = None
    for piece_s, piece_t in zip(block[::2], block[1::2]):
        sim = nt(rows_s, piece_s[...]) - nt(rows_t, piece_t[...])
        term = nn(jnp.tanh(stretch * sim).astype(BF16), piece_s[...])
        total = term if total is None else total + term
    return total


def own_kernel(student, teacher, unit_s, unit_t, scale):
    values = student[...].astype(F32)
    inverse = inverse_rms(values)
    unit_s[...] = (values * inverse * values.shape[-1] ** (-0.5)).astype(BF16)
    unit_t[...] = unit_of(teacher[...])
    scale[...] = jnp.broadcast_to(inverse, scale.shape)


def early_kernel(own_s, own_t, *refs):
    *raws, early_s, early_t, pull = refs
    rows = own_s.shape[0]
    more = early_s.shape[0] - rows
    early_s[pl.ds(0, rows), :] = own_s[...]
    early_t[pl.ds(0, rows), :] = own_t[...]
    at = pl.ds(rows, more)
    store_units((early_s.at[at, :], early_t.at[at, :]), raws)
    pull[...] = pull_of(own_s[...], own_t[...], early_s, early_t)


def mid_kernel(own_s, own_t, before, *refs):
    *raws, mid_s, mid_t, pull = refs
    store_units((mid_s, mid_t), raws)
    pull[...] = before[...] + pull_of(own_s[...], own_t[...], mid_s, mid_t)


def lift_kernel(early_s, mid_s, *refs):
    *raws, once_s, early_p, mid_p = refs
    store_units((once_s,), raws)
    early_p[...] = nt(early_s[...], once_s[...])
    mid_p[...] = nt(mid_s[...], once_s[...])


def late_kernel(once_s, *refs):
    *raws, late_s, late_t, late_p = refs
    store_units((late_s, late_t), raws)
    late_p[...] = nt(late_s[...], once_s[...])


def once_kernel(early_t, mid_t, late_t, early_p, mid_p, late_p, *refs):
    *raws, kept, sent = refs
    stretch = 0.5 * early_t.shape[1] ** 0.5
    once_t = jnp.concatenate([unit_of(r[...]) for r in raws], axis=0)
    first = early_t.shape[0]
    skip = kept.shape[0] - first
    for piece, product, out in (
        (mid_t[...], mid_p[...], sent.at[pl.ds(0, first), :]),
        (early_t[...], early_p[...], kept.at[pl.ds(0, first), :]),
    ):
        out[...] = jnp.tanh(stretch * (product - nt(piece, once_t))).astype(BF16)
    part = jnp.tanh(stretch * (late_p[...] - nt(late_t[...], once_t))).astype(BF16)
    kept[pl.ds(first, skip), :] = part[:skip]
    sent[pl.ds(first, skip), :] = part[skip:]


def back_kernel(early_s, mid_s, late_s, kept, sent, *back):
    first = early_s.shape[0]
    skip = kept.shape[0] - first
    sums = tn(kept[pl.ds(0, first), :], early_s[...]) + tn(sent[pl.ds(0, first), :], mid_s[...])
    last = jnp.concatenate([kept[pl.ds(first, skip), :], sent[pl.ds(first, skip), :]], axis=0)
    sums += tn(last, late_s[...])
    rows = back[0].shape[0]
    for i, out in enumerate(back):
        out[...] = sums[i * rows : (i + 1) * rows].astype(BF16)


def both_kernel(n_both, *refs):
    block, raw_s, raw_t, back = refs[:6], refs[6 : 6 + n_both], refs[6 + n_both : -n_both], refs[-n_both:]
    for i in range(n_both):
        back[i][...] = pull_of(unit_of(raw_s[i][...]), unit_of(raw_t[i][...]), *block).astype(BF16)


def near_kernel(own_s, own_t, late_s, late_t, before, pull):
    pull[...] = before[...] + pull_of(own_s[...], own_t[...], late_s, late_t)


def pack_kernel(kept, came, *outs):
    rows, cols = outs[0].shape
    for k, out in enumerate(outs):
        at = pl.ds(k * rows, rows)
        out[:, pl.ds(0, cols // 2)] = kept[at, :]
        out[:, pl.ds(cols // 2, cols // 2)] = came[at, :]


def met_kernel(n, before, *refs):
    weights, units, pull = refs[:n], refs[n:-1], refs[-1]
    total = before[...]
    for k, weight in enumerate(weights):
        block = jnp.concatenate([units[2 * k][...], units[2 * k + 1][...]], axis=0)
        total += nn(weight[...], block)
    pull[...] = total


def end_kernel(factor, own_s, scale, *refs):
    *terms, out = refs
    unit = own_s[...].astype(F32)
    pull = terms[0][...]
    for term in terms[1:]:
        pull = pull + term[...].astype(F32)
    radial = jnp.sum(unit * pull, axis=-1, keepdims=True)
    out[...] = factor * scale[:, :1] * (pull - radial * unit)


def local(n_gr, n_gc, student, teacher):
    rows, width = student.shape
    axes = ("gr", "gc")

    def shift(x, pairs):
        return lax.ppermute(x, axes, pairs)

    def across(x, mask):
        pairs = [(g * n_gc + c, g * n_gc + (c ^ mask)) for g in range(n_gr) for c in range(n_gc)]
        return shift(x, pairs)

    order = []
    for i in range(n_gr):
        order.append(i // 2 if i % 2 == 0 else n_gr - 1 - i // 2)

    def along(x, step):
        pairs = []
        for i in range(n_gr):
            a, b = order[i], order[(i + step) % n_gr]
            pairs += [(a * n_gc + c, b * n_gc + c) for c in range(n_gc)]
        return shift(x, pairs)

    def run(kernel, outs, *args, flops=0):
        return call(kernel, outs, *args, flops=flops)

    once = list(range(1, (n_gr + 1) // 2))
    both = [n_gr // 2] if n_gr % 2 == 0 else []
    n_once, n_both = len(once), len(both)
    once_rows = n_once * rows
    far_s = [along(student, d) for d in once + both]
    far_t = [along(teacher, d) for d in once + both]

    even = list(range(0, n_gc, 2))
    early = [k for k in even if k & (k - 1) == 0]
    late = [k for k in even if k not in early]
    mid = [k + 1 for k in early]
    last = late + [k + 1 for k in late]
    half = rows * len(even)
    work = 2 * rows * width

    got_s, got_t = {0: student}, {0: teacher}
    for k in even[1:]:
        high = 1 << (k.bit_length() - 1)
        low = k & -k
        got_s[k] = across(got_s[k ^ high], high)
        got_t[k] = across(got_t[k ^ low], low)
    for k in even:
        got_s[k + 1] = across(got_s[k], 1)
        got_t[k + 1] = across(got_t[k], 1)

    def raws(slots):
        return [got_s[k] for k in slots] + [got_t[k] for k in slots]

    pull_shape = shape(rows, width, F32)
    own_s, own_t, scale = run(
        own_kernel, [shape(rows, width, BF16)] * 2 + [shape(rows, 128, F32)], student, teacher
    )
    early_s, early_t, pull = run(
        early_kernel,
        [shape(len(early) * rows, width, BF16)] * 2 + [pull_shape],
        own_s,
        own_t,
        *raws(early[1:]),
        flops=3 * len(early) * rows * work,
    )
    mid_s, mid_t, pull = run(
        mid_kernel,
        [shape(len(mid) * rows, width, BF16)] * 2 + [pull_shape],
        own_s,
        own_t,
        pull,
        *raws(mid),
        flops=3 * len(mid) * rows * work,
    )

    once_s, early_p, mid_p = run(
        lift_kernel,
        [shape(once_rows, width, BF16)] + [shape(len(early) * rows, once_rows, F32)] * 2,
        early_s,
        mid_s,
        *far_s[:n_once],
        flops=2 * len(early) * once_rows * work,
    )
    mates = {0: once_s}
    for k in even[1:]:
        mates[k] = across(once_s, k)
    for k in even:
        mates[k + 1] = across(mates[k], 1)

    late_s, late_t, late_p = run(
        late_kernel,
        [shape(len(last) * rows, width, BF16)] * 2 + [shape(len(last) * rows, once_rows, F32)],
        once_s,
        *raws(last),
        flops=len(last) * once_rows * work,
    )
    kept, sent = run(
        once_kernel,
        [shape(half, once_rows, BF16)] * 2,
        early_t,
        mid_t,
        late_t,
        early_p,
        mid_p,
        late_p,
        *far_t[:n_once],
        flops=n_gc * once_rows * work,
    )
    came = across(sent, 1)
    back = run(
        back_kernel,
        [shape(rows, width, BF16)] * n_once,
        early_s,
        mid_s,
        late_s,
        kept,
        sent,
        flops=n_gc * once_rows * work,
    )
    home = [along(b, n_gr - d) for b, d in zip(back, once)]
    packed = run(pack_kernel, [shape(rows, 2 * once_rows, BF16)] * len(even), kept, came)
    order_of = early + late
    weights = [packed[0]] + [across(p, k) for p, k in zip(packed[1:], order_of[1:])]
    back = run(
        functools.partial(both_kernel, n_both),
        [shape(rows, width, BF16)] * n_both,
        early_s,
        early_t,
        mid_s,
        mid_t,
        late_s,
        late_t,
        *far_s[n_once:],
        *far_t[n_once:],
        flops=3 * n_both * n_gc * rows * work,
    )
    home += [along(b, n_gr - d) for b, d in zip(back, both)]
    (pull,) = run(
        near_kernel,
        [pull_shape],
        own_s,
        own_t,
        late_s,
        late_t,
        pull,
        flops=3 * len(last) * rows * work,
    )
    (pull,) = run(
        functools.partial(met_kernel, len(even)),
        [pull_shape],
        pull,
        *weights,
        *[mates[k + c] for k in order_of for c in (0, 1)],
        flops=n_gc * once_rows * work,
    )
    factor = 12.0 * (width / (rows * n_gr * n_gc)) ** 0.5
    return run(functools.partial(end_kernel, factor), [pull_shape], own_s, scale, pull, *home)[0]


def solution(mesh):
    n_gr, n_gc = mesh.shape["gr"], mesh.shape["gc"]
    spec = P(("gr", "gc"), None)

    def body(student, teacher):
        return local(n_gr, n_gc, student, teacher)

    return jax.shard_map(
        body, mesh=mesh, in_specs=(spec, spec), out_specs=spec, check_vma=False
    )
```

time: 74.4 us -> 82.6 us (1.11)
  starting transfers between devices: 17.4 us -> 24.5 us
  Pallas kernels: 6.61 us -> 9.06 us
  waiting for transfers between devices: 48.2 us -> 46.6 us
    ppermute x23 -> x31, starting transfers between devices: 17.4 us -> 24.5 us  [shift(): return lax.ppermute(x, axes, pairs)]
    pallas_call x4 -> x12, Pallas kernels: 6.61 us -> 9.06 us  [call(): pl.pallas_call(kernel, out_shape=outs, in_specs=[VM] * len(args), out_spe...]
    ppermute x23 -> x31, waiting for transfers between devices: 48.2 us -> 46.6 us  [shift(): return lax.ppermute(x, axes, pairs)]
  transfers between devices with their start and end apart: 23 -> 31, of which waited for: 14 -> 12; matrix products, arithmetic and copies ran while one was open for 0% -> 0% of each run, Pallas kernels for 4% -> 10%
where the time goes in v1:
time: 82.6 us; the launch traced here: 82.4 us
  waiting for transfers between devices  46.6 us (56%)
  starting transfers between devices  24.5 us (30%)
  Pallas kernels  9.06 us (11%)
  local copies, waits for them, and re-layouts  1.98 us (2%)
    ppermute x31, waiting for transfers between devices, shift(): return lax.ppermute(x, axes, pairs)  46.6 us
    ppermute x31, starting transfers between devices, shift(): return lax.ppermute(x, axes, pairs)  24.5 us
    pallas_call x12, Pallas kernels, call(): pl.pallas_call(kernel, out_shape=outs, in_specs=[VM] * len(args), out_spe...  9.06 us
    unnamed x6, local copies, waits for them, and re-layouts  1.98 us
  transfers between devices with their start and end apart: 31, of which 12 were waited for; matrix products, arithmetic and copies ran while one was open for 0% of the time, Pallas kernels for 10%

profile of v1, /device:TPU:0, one launch (start us, length us, event | category | flops | bytes accessed | tf_op | source)
XLA Modules:
  0.0 82.4 jit_solution(4787455021226552908)
XLA Ops:
  0.0 3.0 %collective-permute-start = (bf16[128,1024]{1,0:T(8,128)(2,1)}, bf16[128,1024]{1,0:T(8,128)(2,1)S(1)}, u32[]{:S(2)}, u32[]{:S(2)}) collective-permute-start(bf16[128,1024]{1,0:T(8,128)(2,1)} %student.1), channel_id=1, source_target_pairs={{0,2},{1,3},{2,0},{3,1},{4,6},{5,7},{6,4},{7,5},{8,10},{9,11},{10,... | collective-permute-start | bytes 786440 | tf_op jit(solution)/shard_map/ppermute | solution.py:177
  3.0 1.5 %collective-permute-start.3 = (bf16[128,1024]{1,0:T(8,128)(2,1)}, bf16[128,1024]{1,0:T(8,128)(2,1)S(1)}, u32[]{:S(2)}, u32[]{:S(2)}) collective-permute-start(bf16[128,1024]{1,0:T(8,128)(2,1)} %teacher.1), channel_id=1, source_target_pairs={{0,4},{1,5},{2,6},{3,7},{4,0},{5,1},{6,2},{7,3},{8,12},{9,13},{10,... | collective-permute-start | bytes 786440 | tf_op jit(solution)/shard_map/ppermute | solution.py:177
  5.1 5.3 %collective-permute-done.refs_0_ = bf16[128,1024]{1,0:T(8,128)(2,1)S(1)} collective-permute-done((bf16[128,1024]{1,0:T(8,128)(2,1)}, bf16[128,1024]{1,0:T(8,128)(2,1)S(1)}, u32[]{:S(2)}, u32[]{:S(2)}) %collective-permute-start) | collective-permute-done | bytes 262176 | tf_op jit(solution)/shard_map/ppermute | solution.py:177
  10.3 2.0 %collective-permute-done.3.refs_3_ = bf16[128,1024]{1,0:T(8,128)(2,1)S(1)} collective-permute-done((bf16[128,1024]{1,0:T(8,128)(2,1)}, bf16[128,1024]{1,0:T(8,128)(2,1)S(1)}, u32[]{:S(2)}, u32[]{:S(2)}) %collective-permute-start.3) | collective-permute-done | bytes 262176 | tf_op jit(solution)/shard_map/ppermute | solution.py:177
  12.4 4.2 %collective-permute-done.1.refs_1_ = bf16[128,1024]{1,0:T(8,128)(2,1)S(1)} collective-permute-done((bf16[128,1024]{1,0:T(8,128)(2,1)}, bf16[128,1024]{1,0:T(8,128)(2,1)S(1)}, u32[]{:S(2)}, u32[]{:S(2)}) %collective-permute-start.1) | collective-permute-done | bytes 262176 | tf_op jit(solution)/shard_map/ppermute | solution.py:177
  16.6 1.5 %collective-permute-start.11 = (bf16[128,1024]{1,0:T(8,128)(2,1)S(1)}, bf16[128,1024]{1,0:T(8,128)(2,1)S(1)}, u32[]{:S(2)}, u32[]{:S(2)}) collective-permute-start(bf16[128,1024]{1,0:T(8,128)(2,1)S(1)} %collective-permute-done.refs_0_), channel_id=1, source_target_pairs={{0,4},{1,5},{2,6},{3,7},{4,0},{5,1},{6,2},{7,3},{8,12},{9,13},{10,... | collective-permute-start | bytes 786440 | tf_op jit(solution)/shard_map/ppermute | solution.py:177
  18.1 0.5 collective-permute-start.13
  19.2 3.6 %collective-permute-start.10 = (bf16[128,1024]{1,0:T(8,128)(2,1)}, bf16[128,1024]{1,0:T(8,128)(2,1)S(1)}, u32[]{:S(2)}, u32[]{:S(2)}) collective-permute-start(bf16[128,1024]{1,0:T(8,128)(2,1)} %student.1), channel_id=1, source_target_pairs={{0,24},{1,25},{2,26},{3,27},{4,28},{5,29},{6,30},{7,31},{24,8},{25... | collective-permute-start | bytes 786440 | tf_op jit(solution)/shard_map/ppermute | solution.py:177
  22.8 2.5 %collective-permute-done.11.refs_0_ = bf16[128,1024]{1,0:T(8,128)(2,1)S(1)} collective-permute-done((bf16[128,1024]{1,0:T(8,128)(2,1)S(1)}, bf16[128,1024]{1,0:T(8,128)(2,1)S(1)}, u32[]{:S(2)}, u32[]{:S(2)}) %collective-permute-start.11) | collective-permute-done | bytes 262176 | tf_op jit(solution)/shard_map/ppermute | solution.py:177
  25.3 1.2 %collective-permute-done.13.refs_2_ = bf16[128,1024]{1,0:T(8,128)(2,1)S(1)} collective-permute-done((bf16[128,1024]{1,0:T(8,128)(2,1)S(1)}, bf16[128,1024]{1,0:T(8,128)(2,1)S(1)}, u32[]{:S(2)}, u32[]{:S(2)}) %collective-permute-start.13) | collective-permute-done | bytes 262176 | tf_op jit(solution)/shard_map/ppermute | solution.py:177
  26.5 3.6 %collective-permute-start.15 = (bf16[128,1024]{1,0:T(8,128)(2,1)}, bf16[128,1024]{1,0:T(8,128)(2,1)S(1)}, u32[]{:S(2)}, u32[]{:S(2)}) collective-permute-start(bf16[128,1024]{1,0:T(8,128)(2,1)} %teacher.1), channel_id=1, source_target_pairs={{0,24},{1,25},{2,26},{3,27},{4,28},{5,29},{6,30},{7,31},{24,8},{25... | collective-permute-start | bytes 786440 | tf_op jit(solution)/shard_map/ppermute | solution.py:177
  30.2 1.0 %copy-done = bf16[128,1024]{1,0:T(8,128)(2,1)S(1)} copy-done((bf16[128,1024]{1,0:T(8,128)(2,1)S(1)}, bf16[128,1024]{1,0:T(8,128)(2,1)}, u32[]{:S(2)}) %copy-start) | copy-done | bytes 262168
  31.1 0.9 %copy-done.1 = bf16[128,1024]{1,0:T(8,128)(2,1)S(1)} copy-done((bf16[128,1024]{1,0:T(8,128)(2,1)S(1)}, bf16[128,1024]{1,0:T(8,128)(2,1)}, u32[]{:S(2)}) %copy-start.1) | copy-done | bytes 262168
  32.3 1.0 %shard_map.29 = (bf16[384,1024]{1,0:T(8,128)(2,1)S(1)}, bf16[384,1024]{1,0:T(8,128)(2,1)S(1)}, f32[128,1024]{1,0:T(8,128)S(1)}) custom-call(bf16[128,1024]{1,0:T(8,128)(2,1)S(1)} %get-tuple-element.26.own_s, bf16[128,1024]{1,0:T(8,128)(2,1)S(1)} %get-tuple-element.28.own_t, bf16[128,1024]{1,0:T(8,128)(2,1)S(1)} %collective-permute-done.refs_0_, ...), custom_call_target="tpu_custom_call" | custom-call | flops 301989888 | bytes 3670016 | tf_op jit(solution)/shard_map/pallas_call | solution.py:39
  33.3 1.2 %shard_map.30 = (bf16[384,1024]{1,0:T(8,128)(2,1)S(1)}, bf16[384,1024]{1,0:T(8,128)(2,1)S(1)}, f32[128,1024]{1,0:T(8,128)S(1)}) custom-call(bf16[128,1024]{1,0:T(8,128)(2,1)S(1)} %get-tuple-element.26.own_s, bf16[128,1024]{1,0:T(8,128)(2,1)S(1)} %get-tuple-element.28.own_t, f32[128,1024]{1,0:T(8,128)S(1)} %get-tuple-element.30.before, ...), custom_call_target="tpu_custom_call" | custom-call | flops 301989888 | bytes 4718592 | tf_op jit(solution)/shard_map/pallas_call | solution.py:39
  34.5 6.3 %collective-permute-done.10.refs_0_ = bf16[128,1024]{1,0:T(8,128)(2,1)S(1)} collective-permute-done((bf16[128,1024]{1,0:T(8,128)(2,1)}, bf16[128,1024]{1,0:T(8,128)(2,1)S(1)}, u32[]{:S(2)}, u32[]{:S(2)}) %collective-permute-start.10) | collective-permute-done | bytes 262176 | tf_op jit(solution)/shard_map/ppermute | solution.py:177
  40.8 0.7 shard_map.31
  42.0 3.5 %collective-permute-done.15.refs_0_ = bf16[128,1024]{1,0:T(8,128)(2,1)S(1)} collective-permute-done((bf16[128,1024]{1,0:T(8,128)(2,1)}, bf16[128,1024]{1,0:T(8,128)(2,1)S(1)}, u32[]{:S(2)}, u32[]{:S(2)}) %collective-permute-start.15) | collective-permute-done | bytes 262176 | tf_op jit(solution)/shard_map/ppermute | solution.py:177
  45.5 0.8 shard_map.34
  46.5 1.6 %collective-permute-start.21 = (bf16[128,1024]{1,0:T(8,128)(2,1)S(1)}, bf16[128,1024]{1,0:T(8,128)(2,1)S(1)}, u32[]{:S(2)}, u32[]{:S(2)}) collective-permute-start(bf16[128,1024]{1,0:T(8,128)(2,1)S(1)} %get-tuple-element.32.once_s.refs_4_), channel_id=1, source_target_pairs={{0,2},{1,3},{2,0},{3,1},{4,6},{5,7},{6,4},{7,5},{8,10},{9,11},{10,... | collective-permute-start | bytes 786440 | tf_op jit(solution)/shard_map/ppermute | solution.py:177
  48.6 1.5 %collective-permute-start.25 = (bf16[128,1024]{1,0:T(8,128)(2,1)S(1)}, bf16[128,1024]{1,0:T(8,128)(2,1)S(1)}, u32[]{:S(2)}, u32[]{:S(2)}) collective-permute-start(bf16[128,1024]{1,0:T(8,128)(2,1)S(1)} %get-tuple-element.32.once_s.refs_4_), channel_id=1, source_target_pairs={{0,6},{1,7},{2,4},{3,5},{4,2},{5,3},{6,0},{7,1},{8,14},{9,15},{10,... | collective-permute-start | bytes 786440 | tf_op jit(solution)/shard_map/ppermute | solution.py:177
  50.1 5.0 %collective-permute-done.29.refs_7_ = bf16[128,1024]{1,0:T(8,128)(2,1)S(1)} collective-permute-done((bf16[128,1024]{1,0:T(8,128)(2,1)S(1)}, bf16[128,1024]{1,0:T(8,128)(2,1)S(1)}, u32[]{:S(2)}, u32[]{:S(2)}) %collective-permute-start.29) | collective-permute-done | bytes 262176 | tf_op jit(solution)/shard_map/ppermute | solution.py:177
  55.1 1.5 %collective-permute-start.17 = (bf16[128,256]{1,0:T(8,128)(2,1)S(1)}, bf16[128,256]{1,0:T(8,128)(2,1)S(1)}, u32[]{:S(2)}, u32[]{:S(2)}) collective-permute-start(bf16[128,256]{1,0:T(8,128)(2,1)S(1)} %get-tuple-element.44), channel_id=1, source_target_pairs={{0,2},{1,3},{2,0},{3,1},{4,6},{5,7},{6,4},{7,5},{8,10},{9,11},{10,... | collective-permute-start | bytes 196616 | tf_op jit(solution)/shard_map/ppermute | solution.py:177
  57.1 5.5 %collective-permute-done.23.refs_8_ = bf16[128,1024]{1,0:T(8,128)(2,1)S(1)} collective-permute-done((bf16[128,1024]{1,0:T(8,128)(2,1)S(1)}, bf16[128,1024]{1,0:T(8,128)(2,1)S(1)}, u32[]{:S(2)}, u32[]{:S(2)}) %collective-permute-start.23) | collective-permute-done | bytes 262176 | tf_op jit(solution)/shard_map/ppermute | solution.py:177
  62.7 2.0 %shard_map.38 = bf16[128,1024]{1,0:T(8,128)(2,1)S(1)} custom-call(bf16[384,1024]{1,0:T(8,128)(2,1)S(1)} %get-tuple-element.29.early_s.refs_0_, bf16[384,1024]{1,0:T(8,128)(2,1)S(1)} %get-tuple-element.36.early_t.refs_1_, bf16[384,1024]{1,0:T(8,128)(2,1)S(1)} %get-tuple-element.31.mid_s.refs_2_, bf16[384,1024]{1,0:T(8,128)(2,1)S(1)} %get-tuple-element.37.mid_t.refs_3_, ...), custom_call_target="tpu_custom_call" | custom-call | flops 805306368 | bytes 4980736 | tf_op jit(solution)/shard_map/pallas_call | solution.py:39
  65.3 0.5 shard_map.37
  65.8 1.8 %collective-permute-start.30 = (bf16[128,1024]{1,0:T(8,128)(2,1)S(1)}, bf16[128,1024]{1,0:T(8,128)(2,1)S(1)}, u32[]{:S(2)}, u32[]{:S(2)}) collective-permute-start(bf16[128,1024]{1,0:T(8,128)(2,1)S(1)} %shard_map.38), channel_id=1, source_target_pairs={{0,8},{1,9},{2,10},{3,11},{4,12},{5,13},{6,14},{7,15},{24,16},{25,... | collective-permute-start | bytes 786440 | tf_op jit(solution)/shard_map/ppermute | solution.py:177
  67.8 1.6 %collective-permute-start.27 = (bf16[128,1024]{1,0:T(8,128)(2,1)S(1)}, bf16[128,1024]{1,0:T(8,128)(2,1)S(1)}, u32[]{:S(2)}, u32[]{:S(2)}) collective-permute-start(bf16[128,1024]{1,0:T(8,128)(2,1)S(1)} %shard_map.37), channel_id=1, source_target_pairs={{0,16},{1,17},{2,18},{3,19},{4,20},{5,21},{6,22},{7,23},{24,0},{25... | collective-permute-start | bytes 786440 | tf_op jit(solution)/shard_map/ppermute | solution.py:177
  69.4 0.7 shard_map.33.before
  70.5 4.0 %collective-permute-done.30.refs_2_ = bf16[128,1024]{1,0:T(8,128)(2,1)S(1)} collective-permute-done((bf16[128,1024]{1,0:T(8,128)(2,1)S(1)}, bf16[128,1024]{1,0:T(8,128)(2,1)S(1)}, u32[]{:S(2)}, u32[]{:S(2)}) %collective-permute-start.30) | collective-permute-done | bytes 262176 | tf_op jit(solution)/shard_map/ppermute | solution.py:177
  74.6 6.7 %collective-permute-done.27.refs_1_ = bf16[128,1024]{1,0:T(8,128)(2,1)S(1)} collective-permute-done((bf16[128,1024]{1,0:T(8,128)(2,1)S(1)}, bf16[128,1024]{1,0:T(8,128)(2,1)S(1)}, u32[]{:S(2)}, u32[]{:S(2)}) %collective-permute-start.27) | collective-permute-done | bytes 262176 | tf_op jit(solution)/shard_map/ppermute | solution.py:177
  81.3 1.1 %shard_map.39 = f32[128,1024]{1,0:T(8,128)} custom-call(bf16[128,1024]{1,0:T(8,128)(2,1)S(1)} %get-tuple-element.26.own_s, f32[128,128]{1,0:T(8,128)S(1)} %get-tuple-element.27.scale, f32[128,1024]{1,0:T(8,128)S(1)} %shard_map.36.refs_0_, bf16[128,1024]{1,0:T(8,128)(2,1)S(1)} %collective-permute-done.27.refs_1_, ...), custom_call_target="tpu_custom_call" | custom-call | bytes 1900544 | tf_op jit(solution)/shard_map/pallas_call | solution.py:39
  (48 shorter events, 4.3 us)
Async XLA Ops:
  0.0 10.3 %collective-permute-start = (bf16[128,1024]{1,0:T(8,128)(2,1)}, bf16[128,1024]{1,0:T(8,128)(2,1)S(1)}, u32[]{:S(2)}, u32[]{:S(2)}) collective-permute-start(bf16[128,1024]{1,0:T(8,128)(2,1)} %student.1), channel_id=1, source_target_pairs={{0,2},{1,3},{2,0},{3,1},{4,6},{5,7},{6,4},{7,5},{8,10},{9,11},{10,... | collective-permute-start | bytes 786440 | tf_op jit(solution)/shard_map/ppermute | solution.py:177
  3.0 9.4 %collective-permute-start.3 = (bf16[128,1024]{1,0:T(8,128)(2,1)}, bf16[128,1024]{1,0:T(8,128)(2,1)S(1)}, u32[]{:S(2)}, u32[]{:S(2)}) collective-permute-start(bf16[128,1024]{1,0:T(8,128)(2,1)} %teacher.1), channel_id=1, source_target_pairs={{0,4},{1,5},{2,6},{3,7},{4,0},{5,1},{6,2},{7,3},{8,12},{9,13},{10,... | collective-permute-start | bytes 786440 | tf_op jit(solution)/shard_map/ppermute | solution.py:177
  4.5 12.1 %collective-permute-start.1 = (bf16[128,1024]{1,0:T(8,128)(2,1)}, bf16[128,1024]{1,0:T(8,128)(2,1)S(1)}, u32[]{:S(2)}, u32[]{:S(2)}) collective-permute-start(bf16[128,1024]{1,0:T(8,128)(2,1)} %student.1), channel_id=1, source_target_pairs={{0,4},{1,5},{2,6},{3,7},{4,0},{5,1},{6,2},{7,3},{8,12},{9,13},{10,... | collective-permute-start | bytes 786440 | tf_op jit(solution)/shard_map/ppermute | solution.py:177
  5.0 11.6 %collective-permute-start.2 = (bf16[128,1024]{1,0:T(8,128)(2,1)}, bf16[128,1024]{1,0:T(8,128)(2,1)S(1)}, u32[]{:S(2)}, u32[]{:S(2)}) collective-permute-start(bf16[128,1024]{1,0:T(8,128)(2,1)} %teacher.1), channel_id=1, source_target_pairs={{0,2},{1,3},{2,0},{3,1},{4,6},{5,7},{6,4},{7,5},{8,10},{9,11},{10,... | collective-permute-start | bytes 786440 | tf_op jit(solution)/shard_map/ppermute | solution.py:177
  5.0 13.0 %collective-permute-start.4 = (bf16[128,1024]{1,0:T(8,128)(2,1)}, bf16[128,1024]{1,0:T(8,128)(2,1)S(1)}, u32[]{:S(2)}, u32[]{:S(2)}) collective-permute-start(bf16[128,1024]{1,0:T(8,128)(2,1)} %student.1), channel_id=1, source_target_pairs={{0,1},{1,0},{2,3},{3,2},{4,5},{5,4},{6,7},{7,6},{8,9},{9,8},{10,11... | collective-permute-start | bytes 786440 | tf_op jit(solution)/shard_map/ppermute | solution.py:177
  10.3 8.3 %collective-permute-start.7 = (bf16[128,1024]{1,0:T(8,128)(2,1)}, bf16[128,1024]{1,0:T(8,128)(2,1)S(1)}, u32[]{:S(2)}, u32[]{:S(2)}) collective-permute-start(bf16[128,1024]{1,0:T(8,128)(2,1)} %teacher.1), channel_id=1, source_target_pairs={{0,1},{1,0},{2,3},{3,2},{4,5},{5,4},{6,7},{7,6},{8,9},{9,8},{10,11... | collective-permute-start | bytes 786440 | tf_op jit(solution)/shard_map/ppermute | solution.py:177
  12.4 6.3 %collective-permute-start.5 = (bf16[128,1024]{1,0:T(8,128)(2,1)S(1)}, bf16[128,1024]{1,0:T(8,128)(2,1)S(1)}, u32[]{:S(2)}, u32[]{:S(2)}) collective-permute-start(bf16[128,1024]{1,0:T(8,128)(2,1)S(1)} %collective-permute-done.refs_0_), channel_id=1, source_target_pairs={{0,1},{1,0},{2,3},{3,2},{4,5},{5,4},{6,7},{7,6},{8,9},{9,8},{10,11... | collective-permute-start | bytes 786440 | tf_op jit(solution)/shard_map/ppermute | solution.py:177
  16.6 2.6 %collective-permute-start.9 = (bf16[128,1024]{1,0:T(8,128)(2,1)S(1)}, bf16[128,1024]{1,0:T(8,128)(2,1)S(1)}, u32[]{:S(2)}, u32[]{:S(2)}) collective-permute-start(bf16[128,1024]{1,0:T(8,128)(2,1)S(1)} %collective-permute-done.3.refs_3_), channel_id=1, source_target_pairs={{0,1},{1,0},{2,3},{3,2},{4,5},{5,4},{6,7},{7,6},{8,9},{9,8},{10,11... | collective-permute-start | bytes 786440 | tf_op jit(solution)/shard_map/ppermute | solution.py:177
  16.6 8.7 %collective-permute-start.11 = (bf16[128,1024]{1,0:T(8,128)(2,1)S(1)}, bf16[128,1024]{1,0:T(8,128)(2,1)S(1)}, u32[]{:S(2)}, u32[]{:S(2)}) collective-permute-start(bf16[128,1024]{1,0:T(8,128)(2,1)S(1)} %collective-permute-done.refs_0_), channel_id=1, source_target_pairs={{0,4},{1,5},{2,6},{3,7},{4,0},{5,1},{6,2},{7,3},{8,12},{9,13},{10,... | collective-permute-start | bytes 786440 | tf_op jit(solution)/shard_map/ppermute | solution.py:177
  18.1 8.4 %collective-permute-start.13 = (bf16[128,1024]{1,0:T(8,128)(2,1)S(1)}, bf16[128,1024]{1,0:T(8,128)(2,1)S(1)}, u32[]{:S(2)}, u32[]{:S(2)}) collective-permute-start(bf16[128,1024]{1,0:T(8,128)(2,1)S(1)} %collective-permute-done.3.refs_3_), channel_id=1, source_target_pairs={{0,2},{1,3},{2,0},{3,1},{4,6},{5,7},{6,4},{7,5},{8,10},{9,11},{10,... | collective-permute-start | bytes 786440 | tf_op jit(solution)/shard_map/ppermute | solution.py:177
  18.6 7.9 %collective-permute-start.6 = (bf16[128,1024]{1,0:T(8,128)(2,1)S(1)}, bf16[128,1024]{1,0:T(8,128)(2,1)S(1)}, u32[]{:S(2)}, u32[]{:S(2)}) collective-permute-start(bf16[128,1024]{1,0:T(8,128)(2,1)S(1)} %collective-permute-done.1.refs_1_), channel_id=1, source_target_pairs={{0,1},{1,0},{2,3},{3,2},{4,5},{5,4},{6,7},{7,6},{8,9},{9,8},{10,11... | collective-permute-start | bytes 786440 | tf_op jit(solution)/shard_map/ppermute | solution.py:177
  18.6 11.5 %collective-permute-start.8 = (bf16[128,1024]{1,0:T(8,128)(2,1)S(1)}, bf16[128,1024]{1,0:T(8,128)(2,1)S(1)}, u32[]{:S(2)}, u32[]{:S(2)}) collective-permute-start(bf16[128,1024]{1,0:T(8,128)(2,1)S(1)} %collective-permute-done.2.refs_2_), channel_id=1, source_target_pairs={{0,1},{1,0},{2,3},{3,2},{4,5},{5,4},{6,7},{7,6},{8,9},{9,8},{10,11... | collective-permute-start | bytes 786440 | tf_op jit(solution)/shard_map/ppermute | solution.py:177
  19.2 21.6 %collective-permute-start.10 = (bf16[128,1024]{1,0:T(8,128)(2,1)}, bf16[128,1024]{1,0:T(8,128)(2,1)S(1)}, u32[]{:S(2)}, u32[]{:S(2)}) collective-permute-start(bf16[128,1024]{1,0:T(8,128)(2,1)} %student.1), channel_id=1, source_target_pairs={{0,24},{1,25},{2,26},{3,27},{4,28},{5,29},{6,30},{7,31},{24,8},{25... | collective-permute-start | bytes 786440 | tf_op jit(solution)/shard_map/ppermute | solution.py:177
  25.3 16.2 %collective-permute-start.12 = (bf16[128,1024]{1,0:T(8,128)(2,1)S(1)}, bf16[128,1024]{1,0:T(8,128)(2,1)S(1)}, u32[]{:S(2)}, u32[]{:S(2)}) collective-permute-start(bf16[128,1024]{1,0:T(8,128)(2,1)S(1)} %collective-permute-done.11.refs_0_), channel_id=1, source_target_pairs={{0,1},{1,0},{2,3},{3,2},{4,5},{5,4},{6,7},{7,6},{8,9},{9,8},{10,11... | collective-permute-start | bytes 786440 | tf_op jit(solution)/shard_map/ppermute | solution.py:177
  26.5 14.9 %collective-permute-start.14 = (bf16[128,1024]{1,0:T(8,128)(2,1)S(1)}, bf16[128,1024]{1,0:T(8,128)(2,1)S(1)}, u32[]{:S(2)}, u32[]{:S(2)}) collective-permute-start(bf16[128,1024]{1,0:T(8,128)(2,1)S(1)} %collective-permute-done.13.refs_2_), channel_id=1, source_target_pairs={{0,1},{1,0},{2,3},{3,2},{4,5},{5,4},{6,7},{7,6},{8,9},{9,8},{10,11... | collective-permute-start | bytes 786440 | tf_op jit(solution)/shard_map/ppermute | solution.py:177
  26.5 19.0 %collective-permute-start.15 = (bf16[128,1024]{1,0:T(8,128)(2,1)}, bf16[128,1024]{1,0:T(8,128)(2,1)S(1)}, u32[]{:S(2)}, u32[]{:S(2)}) collective-permute-start(bf16[128,1024]{1,0:T(8,128)(2,1)} %teacher.1), channel_id=1, source_target_pairs={{0,24},{1,25},{2,26},{3,27},{4,28},{5,29},{6,30},{7,31},{24,8},{25... | collective-permute-start | bytes 786440 | tf_op jit(solution)/shard_map/ppermute | solution.py:177
  30.1 18.4 %collective-permute-start.28 = (bf16[128,1024]{1,0:T(8,128)(2,1)}, bf16[128,1024]{1,0:T(8,128)(2,1)S(1)}, u32[]{:S(2)}, u32[]{:S(2)}) collective-permute-start(bf16[128,1024]{1,0:T(8,128)(2,1)} %student.1), channel_id=1, source_target_pairs={{0,8},{1,9},{2,10},{3,11},{4,12},{5,13},{6,14},{7,15},{24,16},{25,... | collective-permute-start | bytes 786440 | tf_op jit(solution)/shard_map/ppermute | solution.py:177
  30.1 1.0 %copy-start = (bf16[128,1024]{1,0:T(8,128)(2,1)S(1)}, bf16[128,1024]{1,0:T(8,128)(2,1)}, u32[]{:S(2)}) copy-start(bf16[128,1024]{1,0:T(8,128)(2,1)} %student.1) | copy-start | bytes 786436
  46.3 3.7 %collective-permute-start.16 = (bf16[512,128]{1,0:T(8,128)(2,1)S(1)}, bf16[512,128]{1,0:T(8,128)(2,1)S(1)}, u32[]{:S(2)}, u32[]{:S(2)}) collective-permute-start(bf16[512,128]{1,0:T(8,128)(2,1)S(1)} %get-tuple-element.42.sent), channel_id=1, source_target_pairs={{0,1},{1,0},{2,3},{3,2},{4,5},{5,4},{6,7},{7,6},{8,9},{9,8},{10,11... | collective-permute-start | bytes 393224 | tf_op jit(solution)/shard_map/ppermute | solution.py:177
  46.4 8.7 %collective-permute-start.29 = (bf16[128,1024]{1,0:T(8,128)(2,1)S(1)}, bf16[128,1024]{1,0:T(8,128)(2,1)S(1)}, u32[]{:S(2)}, u32[]{:S(2)}) collective-permute-start(bf16[128,1024]{1,0:T(8,128)(2,1)S(1)} %copy-done.2), channel_id=1, source_target_pairs={{0,8},{1,9},{2,10},{3,11},{4,12},{5,13},{6,14},{7,15},{24,16},{25,... | collective-permute-start | bytes 786440 | tf_op jit(solution)/shard_map/ppermute | solution.py:177
  46.5 10.1 %collective-permute-start.21 = (bf16[128,1024]{1,0:T(8,128)(2,1)S(1)}, bf16[128,1024]{1,0:T(8,128)(2,1)S(1)}, u32[]{:S(2)}, u32[]{:S(2)}) collective-permute-start(bf16[128,1024]{1,0:T(8,128)(2,1)S(1)} %get-tuple-element.32.once_s.refs_4_), channel_id=1, source_target_pairs={{0,2},{1,3},{2,0},{3,1},{4,6},{5,7},{6,4},{7,5},{8,10},{9,11},{10,... | collective-permute-start | bytes 786440 | tf_op jit(solution)/shard_map/ppermute | solution.py:177
  48.0 14.6 %collective-permute-start.23 = (bf16[128,1024]{1,0:T(8,128)(2,1)S(1)}, bf16[128,1024]{1,0:T(8,128)(2,1)S(1)}, u32[]{:S(2)}, u32[]{:S(2)}) collective-permute-start(bf16[128,1024]{1,0:T(8,128)(2,1)S(1)} %get-tuple-element.32.once_s.refs_4_), channel_id=1, source_target_pairs={{0,4},{1,5},{2,6},{3,7},{4,0},{5,1},{6,2},{7,3},{8,12},{9,13},{10,... | collective-permute-start | bytes 786440 | tf_op jit(solution)/shard_map/ppermute | solution.py:177
  48.6 16.1 %collective-permute-start.25 = (bf16[128,1024]{1,0:T(8,128)(2,1)S(1)}, bf16[128,1024]{1,0:T(8,128)(2,1)S(1)}, u32[]{:S(2)}, u32[]{:S(2)}) collective-permute-start(bf16[128,1024]{1,0:T(8,128)(2,1)S(1)} %get-tuple-element.32.once_s.refs_4_), channel_id=1, source_target_pairs={{0,6},{1,7},{2,4},{3,5},{4,2},{5,3},{6,0},{7,1},{8,14},{9,15},{10,... | collective-permute-start | bytes 786440 | tf_op jit(solution)/shard_map/ppermute | solution.py:177
  50.1 14.7 %collective-permute-start.20 = (bf16[128,1024]{1,0:T(8,128)(2,1)S(1)}, bf16[128,1024]{1,0:T(8,128)(2,1)S(1)}, u32[]{:S(2)}, u32[]{:S(2)}) collective-permute-start(bf16[128,1024]{1,0:T(8,128)(2,1)S(1)} %get-tuple-element.32.once_s.refs_4_), channel_id=1, source_target_pairs={{0,1},{1,0},{2,3},{3,2},{4,5},{5,4},{6,7},{7,6},{8,9},{9,8},{10,11... | collective-permute-start | bytes 786440 | tf_op jit(solution)/shard_map/ppermute | solution.py:177
  55.1 10.1 %collective-permute-start.17 = (bf16[128,256]{1,0:T(8,128)(2,1)S(1)}, bf16[128,256]{1,0:T(8,128)(2,1)S(1)}, u32[]{:S(2)}, u32[]{:S(2)}) collective-permute-start(bf16[128,256]{1,0:T(8,128)(2,1)S(1)} %get-tuple-element.44), channel_id=1, source_target_pairs={{0,2},{1,3},{2,0},{3,1},{4,6},{5,7},{6,4},{7,5},{8,10},{9,11},{10,... | collective-permute-start | bytes 196616 | tf_op jit(solution)/shard_map/ppermute | solution.py:177
  56.6 9.2 %collective-permute-start.18 = (bf16[128,256]{1,0:T(8,128)(2,1)S(1)}, bf16[128,256]{1,0:T(8,128)(2,1)S(1)}, u32[]{:S(2)}, u32[]{:S(2)}) collective-permute-start(bf16[128,256]{1,0:T(8,128)(2,1)S(1)} %get-tuple-element.45), channel_id=1, source_target_pairs={{0,4},{1,5},{2,6},{3,7},{4,0},{5,1},{6,2},{7,3},{8,12},{9,13},{10,... | collective-permute-start | bytes 196616 | tf_op jit(solution)/shard_map/ppermute | solution.py:177
  62.6 5.2 %collective-permute-start.19 = (bf16[128,256]{1,0:T(8,128)(2,1)S(1)}, bf16[128,256]{1,0:T(8,128)(2,1)S(1)}, u32[]{:S(2)}, u32[]{:S(2)}) collective-permute-start(bf16[128,256]{1,0:T(8,128)(2,1)S(1)} %get-tuple-element.46), channel_id=1, source_target_pairs={{0,6},{1,7},{2,4},{3,5},{4,2},{5,3},{6,0},{7,1},{8,14},{9,15},{10,... | collective-permute-start | bytes 196616 | tf_op jit(solution)/shard_map/ppermute | solution.py:177
  64.6 5.4 %collective-permute-start.22 = (bf16[128,1024]{1,0:T(8,128)(2,1)S(1)}, bf16[128,1024]{1,0:T(8,128)(2,1)S(1)}, u32[]{:S(2)}, u32[]{:S(2)}) collective-permute-start(bf16[128,1024]{1,0:T(8,128)(2,1)S(1)} %collective-permute-done.21.refs_6_), channel_id=1, source_target_pairs={{0,1},{1,0},{2,3},{3,2},{4,5},{5,4},{6,7},{7,6},{8,9},{9,8},{10,11... | collective-permute-start | bytes 786440 | tf_op jit(solution)/shard_map/ppermute | solution.py:177
  64.7 5.3 %collective-permute-start.24 = (bf16[128,1024]{1,0:T(8,128)(2,1)S(1)}, bf16[128,1024]{1,0:T(8,128)(2,1)S(1)}, u32[]{:S(2)}, u32[]{:S(2)}) collective-permute-start(bf16[128,1024]{1,0:T(8,128)(2,1)S(1)} %collective-permute-done.23.refs_8_), channel_id=1, source_target_pairs={{0,1},{1,0},{2,3},{3,2},{4,5},{5,4},{6,7},{7,6},{8,9},{9,8},{10,11... | collective-permute-start | bytes 786440 | tf_op jit(solution)/shard_map/ppermute | solution.py:177
  65.2 4.9 %collective-permute-start.26 = (bf16[128,1024]{1,0:T(8,128)(2,1)S(1)}, bf16[128,1024]{1,0:T(8,128)(2,1)S(1)}, u32[]{:S(2)}, u32[]{:S(2)}) collective-permute-start(bf16[128,1024]{1,0:T(8,128)(2,1)S(1)} %collective-permute-done.25.refs_10_), channel_id=1, source_target_pairs={{0,1},{1,0},{2,3},{3,2},{4,5},{5,4},{6,7},{7,6},{8,9},{9,8},{10,11... | collective-permute-start | bytes 786440 | tf_op jit(solution)/shard_map/ppermute | solution.py:177
  65.8 8.7 %collective-permute-start.30 = (bf16[128,1024]{1,0:T(8,128)(2,1)S(1)}, bf16[128,1024]{1,0:T(8,128)(2,1)S(1)}, u32[]{:S(2)}, u32[]{:S(2)}) collective-permute-start(bf16[128,1024]{1,0:T(8,128)(2,1)S(1)} %shard_map.38), channel_id=1, source_target_pairs={{0,8},{1,9},{2,10},{3,11},{4,12},{5,13},{6,14},{7,15},{24,16},{25,... | collective-permute-start | bytes 786440 | tf_op jit(solution)/shard_map/ppermute | solution.py:177
  67.8 13.5 %collective-permute-start.27 = (bf16[128,1024]{1,0:T(8,128)(2,1)S(1)}, bf16[128,1024]{1,0:T(8,128)(2,1)S(1)}, u32[]{:S(2)}, u32[]{:S(2)}) collective-permute-start(bf16[128,1024]{1,0:T(8,128)(2,1)S(1)} %shard_map.37), channel_id=1, source_target_pairs={{0,16},{1,17},{2,18},{3,19},{4,20},{5,21},{6,22},{7,23},{24,0},{25... | collective-permute-start | bytes 786440 | tf_op jit(solution)/shard_map/ppermute | solution.py:177
  (2 other events, 1.9 us)
